TPU v7x, 256 devices: a whole 4x4x8 slice. The times are simulated.
256 devices in a mesh: pb: 16 (over x, z_hi), sa: 16 (over z_lo, y, core).
Axes of the slice: x: 4, y: 4, z: 8 (z_hi: 4, z_lo: 2; z = z_hi * 2 + z_lo), core: 2. Of those that a mesh axis runs over, the one named last changes fastest.
Arguments:
- question_states: bfloat16 [16, 16, 256, 768], P('pb', 'sa'), may hold values from -16 to 16
- question_ids: int32 [16, 16, 256], P('pb'), may hold values from 0 to 30521, as said below
- q_inner_weight: bfloat16 [768, 3072], P(None, 'sa'), may hold values from -0.21875 to 0.21875
- q_outer_weight: bfloat16 [3072, 768], P('sa'), may hold values from -0.109375 to 0.109375
- q_norm_gain: float32 [768], replicated, may hold values from 0.1 to 1.9
- sql_states: bfloat16 [16, 16, 256, 768], P('sa', 'pb'), may hold values from -16 to 16
- sql_ids: int32 [16, 16, 256], P('sa'), may hold values from 0 to 32099, as said below
- s_inner_weight: bfloat16 [768, 3072], P(None, 'pb'), may hold values from -0.21875 to 0.21875
- s_outer_weight: bfloat16 [3072, 768], P('pb'), may hold values from -0.109375 to 0.109375
- s_norm_gain: float32 [768], replicated, may hold values from 0.1 to 1.9
- positive_column: int32 [256], P('pb'), may hold values from 0 to 255, each once
Outputs:
- loss: float32 [], replicated
- q_inner_grad: float32 [768, 3072], P(None, 'sa')
- q_outer_grad: float32 [3072, 768], P('sa')
- q_gain_grad: float32 [768], replicated
- s_inner_grad: float32 [768, 3072], P(None, 'pb')
- s_outer_grad: float32 [3072, 768], P('pb')
- s_gain_grad: float32 [768], replicated
Inputs may be any that keep to these rules, and one draw needn't show every extreme that they name: `question_ids`: each sequence is a run of nonzero ids followed by padding zeros, the run 3 * 64 long or longer. `sql_ids`: each sequence is a run of nonzero ids followed by padding zeros, the run 3 * 64 long or longer.
All inputs are finite; a program needn't handle non-finite values.
Results may differ from a plain program's by a relative error of at most 0.0051.
Values may be sent and summed in bfloat16 or wider, within the bound.
A program may use at most 128 MiB of HBM per device.

v0:
```python
import math
import jax
import jax.numpy as jnp
from jax import lax
from jax.sharding import PartitionSpec as P

D = 768
HIGH = lax.Precision.HIGHEST


def apply_rms_norm(input_float, norm_gain_vector, root_mean_square):
    if root_mean_square:
        input_normalized = input_float * lax.rsqrt(
            jnp.mean(input_float * input_float, axis=-1, keepdims=True) + 1e-06
        )
    else:
        mean_removed = input_float - jnp.mean(input_float, axis=-1, keepdims=True)
        input_normalized = mean_removed * lax.rsqrt(
            jnp.mean(mean_removed * mean_removed, axis=-1, keepdims=True) + 1e-05
        )
    return (input_normalized, (input_normalized * norm_gain_vector).astype(jnp.bfloat16))


def gelu_value(v):
    return 0.5 * v * (1.0 + lax.erf(v / math.sqrt(2.0)))


def gelu_slope(v):
    return 0.5 * (1.0 + lax.erf(v / math.sqrt(2.0))) + v * jnp.exp(-0.5 * v * v) / math.sqrt(
        2.0 * math.pi
    )


def pool_weights(ids):
    mask = (ids > 0).astype(jnp.float32)
    return mask / jnp.sum(mask, axis=-1, keepdims=True)


def tower_forward(tokens, ids, inner, gain, root_mean_square):
    count, length, width = tokens.shape
    input_float = tokens.astype(jnp.float32).reshape(count * length, width)
    input_normalized, normalized_rows = apply_rms_norm(input_float, gain, root_mean_square)
    pre = jnp.dot(normalized_rows, inner, preferred_element_type=jnp.float32)
    weights = pool_weights(ids)
    hidden = gelu_value(pre).reshape(count, length, -1)
    pooled = jnp.einsum("nt,ntf->nf", weights, hidden, precision=HIGH)
    resid = jnp.einsum(
        "nt,ntd->nd", weights, input_float.reshape(count, length, width), precision=HIGH
    )
    return (input_normalized, normalized_rows, pre, weights, pooled, resid)


def tower_backward(input_normalized, normalized_rows, pre, weights, inner, hidden_grad):
    count, length = weights.shape
    slope = gelu_slope(pre).reshape(count, length, -1)
    dpre = (
        (weights[:, :, None] * hidden_grad[:, None, :] * slope)
        .reshape(count * length, -1)
        .astype(jnp.bfloat16)
    )
    inner_part = lax.dot_general(
        normalized_rows, dpre, (((0,), (0,)), ((), ())), preferred_element_type=jnp.float32
    )
    normalized_grad = lax.dot_general(
        dpre, inner, (((1,), (1,)), ((), ())), preferred_element_type=jnp.float32
    )
    return (inner_part, jnp.sum(input_normalized * normalized_grad, axis=0))


def per_device(
    question_states,
    question_ids,
    q_inner_weight,
    q_outer_weight,
    q_norm_gain,
    sql_states,
    sql_ids,
    s_inner_weight,
    s_outer_weight,
    s_norm_gain,
    positive_column,
):
    scale = 1.0 / math.sqrt(D)
    q_place = lax.axis_index("sa")
    s_place = lax.axis_index("pb")
    q_tokens = lax.all_gather(question_states, "sa", axis=1, tiled=True)[0]
    s_tokens = lax.all_gather(sql_states, "pb", axis=1, tiled=True)[0]
    q_rows = q_tokens.shape[0]
    s_rows = s_tokens.shape[0]
    q_hat, q_normed, q_pre, q_weights, q_pooled, q_resid = tower_forward(
        q_tokens, question_ids[0], q_inner_weight, q_norm_gain, False
    )
    s_hat, s_normed, s_pre, s_weights, s_pooled, s_resid = tower_forward(
        s_tokens, sql_ids[0], s_inner_weight, s_norm_gain, True
    )
    q_outer_f = q_outer_weight.astype(jnp.float32)
    s_outer_f = s_outer_weight.astype(jnp.float32)
    q_block = lax.psum(jnp.dot(q_pooled, q_outer_f, precision=HIGH), "sa") + q_resid
    s_block = lax.psum(jnp.dot(s_pooled, s_outer_f, precision=HIGH), "pb") + s_resid
    q_embed = lax.all_gather(q_block, "pb", axis=0, tiled=True)
    s_embed = lax.all_gather(s_block, "sa", axis=0, tiled=True)
    q_pooled_all = lax.all_gather(q_pooled, "pb", axis=0, tiled=True)
    s_pooled_all = lax.all_gather(s_pooled, "sa", axis=0, tiled=True)
    positive_all = lax.all_gather(positive_column, "pb", axis=0, tiled=True)
    score = scale * lax.dot_general(q_embed, s_embed, (((1,), (1,)), ((), ())), precision=HIGH)
    count = score.shape[0]
    match = (positive_all[:, None] == jnp.arange(count, dtype=jnp.int32)[None, :]).astype(
        jnp.float32
    )
    row_max = jnp.max(score, axis=1)
    row_lse = row_max + jnp.log(jnp.sum(jnp.exp(score - row_max[:, None]), axis=1))
    col_max = jnp.max(score, axis=0)
    col_lse = col_max + jnp.log(jnp.sum(jnp.exp(score - col_max[None, :]), axis=0))
    row_pos = jnp.sum(match * score, axis=1)
    col_pos = jnp.sum(match * score, axis=0)
    loss = (jnp.sum(row_lse - row_pos) + jnp.sum(col_lse - col_pos)) / (2.0 * count)
    dscore = 0.5 * (
        jnp.exp(score - row_lse[:, None]) + jnp.exp(score - col_lse[None, :]) - 2.0 * match
    )
    q_grad = scale * jnp.dot(dscore, s_embed, precision=HIGH)
    s_grad = scale * lax.dot_general(dscore, q_embed, (((0,), (0,)), ((), ())), precision=HIGH)
    q_outer_grad = lax.dot_general(q_pooled_all, q_grad, (((0,), (0,)), ((), ())), precision=HIGH)
    s_outer_grad = lax.dot_general(s_pooled_all, s_grad, (((0,), (0,)), ((), ())), precision=HIGH)
    q_grad_own = lax.dynamic_slice_in_dim(q_grad, s_place * q_rows, q_rows, 0)
    s_grad_own = lax.dynamic_slice_in_dim(s_grad, q_place * s_rows, s_rows, 0)
    q_hidden_grad = lax.dot_general(q_grad_own, q_outer_f, (((1,), (1,)), ((), ())), precision=HIGH)
    s_hidden_grad = lax.dot_general(s_grad_own, s_outer_f, (((1,), (1,)), ((), ())), precision=HIGH)
    q_inner_part, q_gain_part = tower_backward(
        q_hat, q_normed, q_pre, q_weights, q_inner_weight, q_hidden_grad
    )
    s_inner_part, s_gain_part = tower_backward(
        s_hat, s_normed, s_pre, s_weights, s_inner_weight, s_hidden_grad
    )
    q_inner_grad = lax.psum(q_inner_part, "pb")
    s_inner_grad = lax.psum(s_inner_part, "sa")
    q_gain_grad, s_gain_grad = lax.psum((q_gain_part, s_gain_part), ("pb", "sa"))
    return (loss, q_inner_grad, q_outer_grad, q_gain_grad, s_inner_grad, s_outer_grad, s_gain_grad)


def solution(mesh):
    placed = (
        P("pb", "sa", None, None),
        P("pb", None, None),
        P(None, "sa"),
        P("sa", None),
        P(),
        P("sa", "pb", None, None),
        P("sa", None, None),
        P(None, "pb"),
        P("pb", None),
        P(),
        P("pb"),
    )
    return jax.shard_map(
        per_device,
        mesh=mesh,
        in_specs=placed,
        out_specs=(P(), P(None, "sa"), P("sa", None), P(), P(None, "pb"), P("pb", None), P()),
        check_vma=False,
    )
```

profile of v0, /device:TPU:25, one launch (start us, length us, event | category | flops | bytes accessed | tf_op | source)
XLA Modules:
  0.0 705.5 jit_solution(16623077752459873952)
XLA Ops:
  14.6 18.9 %all-reduce = s32[256]{0:T(256)} all-reduce(s32[256]{0:T(256)S(1)} %dynamic-update-slice), channel_id=1, replica_groups=mesh['pb'=16,'sa'=16] {'pb'}, use_global_device_ids=true, to_apply=%add | all-reduce | flops 256 | bytes 2048
  33.5 70.1 %all-gather.5.cloned.1.call-done = bf16[1,16,256,768]{3,2,0,1:T(8,128)(2,1)} async-done(((bf16[1,1,256,768]{3,2,0,1:T(8,128)(2,1)}), bf16[1,16,256,768]{3,2,0,1:T(8,128)(2,1)}) %all-gather.5.cloned.1.call-update) | async-done | bytes 6291472 | tf_op jit(solution)/shard_map/all_gather | solution.py:87
  103.6 4.1 multiply_reduce_fusion.2
  107.7 48.2 %all-gather.3.cloned.1.call-done = bf16[1,16,256,768]{3,2,0,1:T(8,128)(2,1)} async-done(((bf16[1,1,256,768]{3,2,0,1:T(8,128)(2,1)}), bf16[1,16,256,768]{3,2,0,1:T(8,128)(2,1)}) %all-gather.3.cloned.1.call-update) | async-done | bytes 6291472 | tf_op jit(solution)/shard_map/all_gather | solution.py:86
  155.9 3.8 convert_reduce_fusion
  164.8 3.8 multiply_multiply_fusion.2
  168.6 2.7 fusion.17
  172.1 69.0 %psum.43 = f32[16,768]{1,0:T(8,128)S(1)} all-reduce(f32[16,768]{1,0:T(8,128)S(1)} %fusion.42), channel_id=1, replica_groups=mesh['pb'=16,'sa'=16] {'pb'}, use_global_device_ids=true, to_apply=%region_6.0 | all-reduce | flops 12288 | bytes 98304 | tf_op jit(solution)/shard_map/psum | solution.py:99
  241.1 5.3 fusion.1
  246.5 32.6 %all_gather.24 = f32[256,768]{1,0:T(8,128)} all-gather(f32[16,768]{1,0:T(8,128)S(1)} %bitcast_add_fusion), channel_id=1, replica_groups=mesh['pb'=16,'sa'=16] {'sa'}, dimensions={0}, use_global_device_ids=true | all-gather | bytes 835584 | tf_op jit(solution)/shard_map/all_gather | solution.py:101
  279.1 4.6 multiply_convert_fusion.1
  289.8 53.6 %psum.42 = f32[16,768]{1,0:T(8,128)S(1)} all-reduce(f32[16,768]{1,0:T(8,128)S(1)} %fusion.41), channel_id=1, replica_groups=mesh['pb'=16,'sa'=16] {'sa'}, use_global_device_ids=true, to_apply=%region_3.0 | all-reduce | flops 12288 | bytes 98304 | tf_op jit(solution)/shard_map/psum | solution.py:98
  343.4 5.4 fusion.3
  348.8 39.3 %all_gather.22 = f32[256,768]{1,0:T(8,128)S(1)} all-gather(f32[16,768]{1,0:T(8,128)S(1)} %bitcast_add_fusion.1), channel_id=1, replica_groups=mesh['pb'=16,'sa'=16] {'pb'}, dimensions={0}, use_global_device_ids=true | all-gather | bytes 835584 | tf_op jit(solution)/shard_map/all_gather | solution.py:100
  393.6 2.7 copy.41
  402.4 4.4 copy.44
  408.2 3.7 fusion.16
  412.2 4.9 multiply_reduce_fusion.1
  417.2 2.8 multiply_reduce_fusion
  420.0 81.8 %all-reduce.1 = (f32[768]{0:T(1024)}, f32[768]{0:T(1024)}) all-reduce(f32[768]{0:T(1024)S(1)} %multiply_reduce_fusion.1, f32[768]{0:T(1024)S(1)} %multiply_reduce_fusion), channel_id=1, replica_groups=mesh['pb'=16,'sa'=16] {'pb','sa'}, use_global_device_ids=true, to_apply=%region_17.0 | all-reduce | flops 1536 | bytes 12288 | tf_op jit(solution)/shard_map/psum | solution.py:136
  501.8 16.7 %all_gather.27 = f32[256,192]{1,0:T(8,128)S(1)} all-gather(f32[16,192]{1,0:T(8,128)S(1)} %bitcast.132), channel_id=1, replica_groups=mesh['pb'=16,'sa'=16] {'sa'}, dimensions={0}, use_global_device_ids=true | all-gather | bytes 208896 | tf_op jit(solution)/shard_map/all_gather | solution.py:103
  518.5 5.5 fusion.47
  524.1 37.7 %all_gather.26 = f32[256,192]{1,0:T(8,128)S(1)} all-gather(f32[16,192]{1,0:T(8,128)S(1)} %bitcast.133), channel_id=1, replica_groups=mesh['pb'=16,'sa'=16] {'pb'}, dimensions={0}, use_global_device_ids=true | all-gather | bytes 208896 | tf_op jit(solution)/shard_map/all_gather | solution.py:102
  564.9 128.9 %all-reduce.7.cloned.1.call-done = f32[768,192]{0,1:T(8,128)} async-done(((f32[768,192]{0,1:T(8,128)}), f32[768,192]{0,1:T(8,128)}) %all-reduce.7.cloned.1.call-update) | async-done | bytes 589840 | tf_op jit(solution)/shard_map/psum | solution.py:135
  (130 shorter events, 37.4 us)
Async XLA Ops:
  7.2 276.5 %copy-start = (bf16[768,192]{0,1:T(8,128)(2,1)S(1)}, bf16[768,192]{0,1:T(8,128)(2,1)}, u32[]{:S(2)}) copy-start(bf16[768,192]{0,1:T(8,128)(2,1)} %param.13) | copy-start | bytes 884740
  7.2 96.4 %all-gather.5.cloned.1.call-start = ((), (), s32[]{:S(2)}) async-start(), calls=%async_computation.1 | async-start | bytes 6684672 | tf_op jit(solution)/shard_map/all_gather | solution.py:87
  7.9 148.0 %all-gather.3.cloned.1.call-start = ((), (), s32[]{:S(2)}) async-start(), calls=%async_computation | async-start | bytes 6684672 | tf_op jit(solution)/shard_map/all_gather | solution.py:86
  8.7 556.3 %all-reduce.5.cloned.1.call-start = ((), (), s32[]{:S(2)}) async-start(), calls=%async_computation.2 | async-start | bytes 1179648 | tf_op jit(solution)/shard_map/psum | solution.py:134
  107.7 54.8 %copy-start.19 = (f32[2,2,8,128]{3,1,2,0:T(2,128)}, f32[2,2,8,128]{3,1,2,0:T(2,128)S(1)}, u32[]{:S(2)}) copy-start(f32[2,2,8,128]{3,1,2,0:T(2,128)S(1)} %copy.38) | copy-start | bytes 49156
  159.8 119.3 %copy-start.21 = (f32[2,2,8,128]{3,1,2,0:T(2,128)}, f32[2,2,8,128]{3,1,2,0:T(2,128)S(1)}, u32[]{:S(2)}) copy-start(f32[2,2,8,128]{3,1,2,0:T(2,128)S(1)} %copy.36) | copy-start | bytes 49156
  162.5 116.6 %copy-start.23 = (f32[2,2,8,128]{3,1,2,0:T(2,128)}, f32[2,2,8,128]{3,1,2,0:T(2,128)S(1)}, u32[]{:S(2)}) copy-start(f32[2,2,8,128]{3,1,2,0:T(2,128)S(1)} %copy.37) | copy-start | bytes 49156
  241.1 38.0 %copy-start.29 = (f32[768]{0:T(1024)S(1)}, f32[768]{0:T(1024)}, u32[]{:S(2)}) copy-start(f32[768]{0:T(1024)} %param.15) | copy-start | bytes 9220
  343.3 44.7 %copy-start.5 = (f32[256,768]{1,0:T(8,128)S(1)}, f32[256,768]{1,0:T(8,128)}, u32[]{:S(2)}) copy-start(f32[256,768]{1,0:T(8,128)} %all_gather.24) | copy-start | bytes 2359300
  343.4 45.7 %copy-start.27 = (s32[256]{0:T(256)S(1)}, s32[256]{0:T(256)}, u32[]{:S(2)}) copy-start(s32[256]{0:T(256)} %all-reduce) | copy-start | bytes 3076
  348.8 43.9 %copy-start.12 = (bf16[192,768]{1,0:T(8,128)(2,1)S(1)}, bf16[192,768]{1,0:T(8,128)(2,1)}, u32[]{:S(2)}) copy-start(bf16[192,768]{1,0:T(8,128)(2,1)} %param.14) | copy-start | bytes 884740
  393.6 5.4 slice-start.4
  401.3 292.6 %all-reduce.7.cloned.1.call-start = ((), (), s32[]{:S(2)}) async-start(), calls=%async_computation.3 | async-start | bytes 1179648 | tf_op jit(solution)/shard_map/psum | solution.py:135
  402.4 5.8 copy-start.17
  402.4 9.5 %slice-start = ((s8[6291456]{0:T(1024)(128)(4,1)}), s8[2097152]{0:T(1024)(128)(4,1)S(1)}, s32[]{:S(2)}) async-start(s8[6291456]{0:T(1024)(128)(4,1)} %bitcast.112), calls=%async_computation.4 | async-start | bytes 4194304
  402.4 9.5 %copy-start.22 = (f32[2,2,8,128]{3,1,2,0:T(2,128)S(1)}, f32[2,2,8,128]{3,1,2,0:T(2,128)}, u32[]{:S(2)}) copy-start(f32[2,2,8,128]{3,1,2,0:T(2,128)} %copy-done.21) | copy-start | bytes 49156
  402.4 9.5 %copy-start.24 = (f32[2,2,8,128]{3,1,2,0:T(2,128)S(1)}, f32[2,2,8,128]{3,1,2,0:T(2,128)}, u32[]{:S(2)}) copy-start(f32[2,2,8,128]{3,1,2,0:T(2,128)} %copy-done.23) | copy-start | bytes 49156
  408.2 9.0 %slice-start.2 = ((s8[6291456]{0:T(1024)(128)(4,1)}), s8[4194304]{0:T(1024)(128)(4,1)S(1)}, s32[]{:S(2)}) async-start(s8[6291456]{0:T(1024)(128)(4,1)} %bitcast.114), calls=%async_computation.6 | async-start | bytes 8388608
  412.2 5.0 slice-start.3
  412.2 5.0 copy-start.16
  412.2 5.0 copy-start.20
  417.2 84.6 %copy-start.25 = (f32[16,1,192]{2,0,1:T(8,128)S(1)}, f32[16,1,192]{2,0,1:T(8,128)}, u32[]{:S(2)}) copy-start(f32[16,1,192]{2,0,1:T(8,128)} %copy.67) | copy-start | bytes 36868
  518.5 5.6 copy-start.26
  518.5 44.9 %copy-start.7 = (f32[256,768]{1,0:T(8,128)S(1)}, f32[256,768]{1,0:T(8,128)}, u32[]{:S(2)}) copy-start(f32[256,768]{1,0:T(8,128)} %copy-done.6) | copy-start | bytes 2359300
  (16 other events, 47.3 us)
Sparse Core Ops, SparseCore 0:
  10.5 93.0 all-gather.4
  105.5 50.4 all-gather.2
  401.4 159.6 all-reduce.4
  564.3 129.4 all-reduce.6
where the time goes:
time: 713 us; the launch traced here: 706 us
  blocking collectives  350 us (49%)
  waiting for transfers between devices  249 us (35%)
  matrix products  45.8 us (6%)
  other arithmetic  25 us (4%)
  local copies, waits for them, and re-layouts  18.6 us (3%)
  between operations  17.6 us (2%)
    psum x1, waiting for transfers between devices, per_device(): s_inner_grad = lax.psum(s_inner_part, 'sa')  129 us
    psum x1, blocking collectives, per_device(): lax.psum((q_gain_part, s_gain_part), ('pb', 'sa'))  81.8 us
    all_gather x1, waiting for transfers between devices, per_device(): s_tokens = lax.all_gather(sql_states, 'pb', axis=1, tiled=True)[0]  70.1 us
    psum x1, blocking collectives, per_device(): lax.psum(jnp.dot(s_pooled, s_outer_f, precision=HIGH), 'pb') + s_resid  69 us
    psum x1, blocking collectives, per_device(): lax.psum(jnp.dot(q_pooled, q_outer_f, precision=HIGH), 'sa') + q_resid  53.6 us
    all_gather x1, waiting for transfers between devices, per_device(): q_tokens = lax.all_gather(question_states, 'sa', axis=1, tiled=True)[0]  48.2 us
    all_gather x1, blocking collectives, per_device(): q_embed = lax.all_gather(q_block, 'pb', axis=0, tiled=True)  39.3 us
    all_gather x1, blocking collectives, per_device(): q_pooled_all = lax.all_gather(q_pooled, 'pb', axis=0, tiled=True)  37.7 us
  transfers between devices with their start and end apart: 4, of which 3 were waited for; matrix products, arithmetic and copies ran while one was open for 5% of the time, Pallas kernels for 0%

commit v1 on v0

--- a/solution.py
+++ b/solution.py
@@ -3,6 +3,7 @@
 import jax.numpy as jnp
 from jax import lax
 from jax.sharding import PartitionSpec as P
+from jax.lax import all_to_all, axis_size
 
 D = 768
 HIGH = lax.Precision.HIGHEST
@@ -98,7 +99,9 @@
     q_block = lax.psum(jnp.dot(q_pooled, q_outer_f, precision=HIGH), "sa") + q_resid
     s_block = lax.psum(jnp.dot(s_pooled, s_outer_f, precision=HIGH), "pb") + s_resid
     q_embed = lax.all_gather(q_block, "pb", axis=0, tiled=True)
-    s_embed = lax.all_gather(s_block, "sa", axis=0, tiled=True)
+    s_embed = jnp.concatenate(
+        all_to_all(jnp.stack([s_block] * axis_size("sa")), "sa", 0, 0), axis=0
+    )
     q_pooled_all = lax.all_gather(q_pooled, "pb", axis=0, tiled=True)
     s_pooled_all = lax.all_gather(s_pooled, "sa", axis=0, tiled=True)
     positive_all = lax.all_gather(positive_column, "pb", axis=0, tiled=True)

time: 713 us -> 770 us (1.080)
  waiting for transfers between devices: 249 us -> 308 us
  blocking collectives: 350 us -> 327 us
  starting transfers between devices: 0.37 us -> 19.4 us
    psum x1, waiting for transfers between devices: 0.01 us -> 55.2 us  [per_device(): q_inner_grad = lax.psum(q_inner_part, 'pb')]
    all_gather x1 -> x0, blocking collectives: 32.6 us -> none  [per_device(): s_embed = lax.all_gather(s_block, 'sa', axis=0, tiled=True)]
    all_to_all x0 -> x1, starting transfers between devices: none -> 19.1 us  [per_device(): all_to_all(jnp.stack([s_block] * axis_size('sa')), 'sa', 0, 0)]
    psum x1, blocking collectives: 81.8 us -> 90.3 us  [per_device(): lax.psum((q_gain_part, s_gain_part), ('pb', 'sa'))]
    unnamed x86 -> x84, local copies, waits for them, and re-layouts: 16.4 us -> 15.6 us
  transfers between devices with their start and end apart: 4 -> 5, of which waited for: 3 -> 4; matrix products, arithmetic and copies ran while one was open for 5% -> 6% of each run, Pallas kernels for 0% -> 0%
where the time goes in v1:
time: 770 us; the launch traced here: 761 us
  blocking collectives  327 us (42%)
  waiting for transfers between devices  308 us (40%)
  matrix products  48.4 us (6%)
  other arithmetic  22.7 us (3%)
  starting transfers between devices  19.4 us (3%)
  local copies, waits for them, and re-layouts  18.8 us (2%)
  between operations  17.6 us (2%)
    psum x1, waiting for transfers between devices, per_device(): s_inner_grad = lax.psum(s_inner_part, 'sa')  133 us
    psum x1, blocking collectives, per_device(): lax.psum((q_gain_part, s_gain_part), ('pb', 'sa'))  90.3 us
    all_gather x1, waiting for transfers between devices, per_device(): s_tokens = lax.all_gather(sql_states, 'pb', axis=1, tiled=True)[0]  70.1 us
    psum x1, blocking collectives, per_device(): lax.psum(jnp.dot(s_pooled, s_outer_f, precision=HIGH), 'pb') + s_resid  69 us
    psum x1, waiting for transfers between devices, per_device(): q_inner_grad = lax.psum(q_inner_part, 'pb')  55.2 us
    psum x1, blocking collectives, per_device(): lax.psum(jnp.dot(q_pooled, q_outer_f, precision=HIGH), 'sa') + q_resid  52.3 us
    all_gather x1, waiting for transfers between devices, per_device(): q_tokens = lax.all_gather(question_states, 'sa', axis=1, tiled=True)[0]  48.2 us
    all_gather x1, blocking collectives, per_device(): q_embed = lax.all_gather(q_block, 'pb', axis=0, tiled=True)  40.2 us
  transfers between devices with their start and end apart: 5, of which 4 were waited for; matrix products, arithmetic and copies ran while one was open for 6% of the time, Pallas kernels for 0%

profile of v1, /device:TPU:25, one launch (start us, length us, event | category | flops | bytes accessed | tf_op | source)
XLA Modules:
  0.0 761.2 jit_solution(293692618471218624)
XLA Ops:
  14.6 18.9 %all-reduce = s32[256]{0:T(256)} all-reduce(s32[256]{0:T(256)S(1)} %dynamic-update-slice), channel_id=1, replica_groups=mesh['pb'=16,'sa'=16] {'pb'}, use_global_device_ids=true, to_apply=%add | all-reduce | flops 256 | bytes 2048
  33.5 70.1 %all-gather.5.cloned.1.call-done = bf16[1,16,256,768]{3,2,0,1:T(8,128)(2,1)} async-done(((bf16[1,1,256,768]{3,2,0,1:T(8,128)(2,1)}), bf16[1,16,256,768]{3,2,0,1:T(8,128)(2,1)}) %all-gather.5.cloned.1.call-update) | async-done | bytes 6291472 | tf_op jit(solution)/shard_map/all_gather | solution.py:88
  103.6 4.1 multiply_reduce_fusion.2
  107.7 48.2 %all-gather.3.cloned.1.call-done = bf16[1,16,256,768]{3,2,0,1:T(8,128)(2,1)} async-done(((bf16[1,1,256,768]{3,2,0,1:T(8,128)(2,1)}), bf16[1,16,256,768]{3,2,0,1:T(8,128)(2,1)}) %all-gather.3.cloned.1.call-update) | async-done | bytes 6291472 | tf_op jit(solution)/shard_map/all_gather | solution.py:87
  155.9 3.8 convert_reduce_fusion
  164.8 3.5 multiply_multiply_fusion.2
  168.3 2.7 fusion.17
  171.9 69.0 %psum.43 = f32[16,768]{1,0:T(8,128)S(1)} all-reduce(f32[16,768]{1,0:T(8,128)S(1)} %fusion.42), channel_id=1, replica_groups=mesh['pb'=16,'sa'=16] {'pb'}, use_global_device_ids=true, to_apply=%region_6.0 | all-reduce | flops 12288 | bytes 98304 | tf_op jit(solution)/shard_map/psum | solution.py:100
  240.8 5.4 fusion.1
  247.2 19.1 %all-to-all-start = ((f32[16,16,768]{2,1,0:T(8,128)}), f32[16,16,768]{2,1,0:T(8,128)}, u32[]{:S(2)}, u32[]{:S(2)}) async-start(f32[16,16,768]{2,1,0:T(8,128)} %stack.2), calls=%async_computation | async-start | bytes 1572864 | tf_op jit(solution)/shard_map/all_to_all | solution.py:103
  266.3 4.6 multiply_convert_fusion.1
  270.9 3.7 multiply_multiply_fusion.3
  278.2 52.3 %psum.42 = f32[16,768]{1,0:T(8,128)S(1)} all-reduce(f32[16,768]{1,0:T(8,128)S(1)} %fusion.41), channel_id=1, replica_groups=mesh['pb'=16,'sa'=16] {'sa'}, use_global_device_ids=true, to_apply=%region_3.0 | all-reduce | flops 12288 | bytes 98304 | tf_op jit(solution)/shard_map/psum | solution.py:99
  330.5 20.7 %all_gather.23 = f32[256,192]{1,0:T(8,128)} all-gather(f32[16,192]{1,0:T(8,128)} %bitcast.135), channel_id=1, replica_groups=mesh['pb'=16,'sa'=16] {'sa'}, dimensions={0}, use_global_device_ids=true | all-gather | bytes 208896 | tf_op jit(solution)/shard_map/all_gather | solution.py:106
  351.2 35.3 %all_gather.22 = f32[256,192]{1,0:T(8,128)} all-gather(f32[16,192]{1,0:T(8,128)} %bitcast.138), channel_id=1, replica_groups=mesh['pb'=16,'sa'=16] {'pb'}, dimensions={0}, use_global_device_ids=true | all-gather | bytes 208896 | tf_op jit(solution)/shard_map/all_gather | solution.py:105
  386.4 5.3 fusion.3
  391.8 40.2 %all_gather.19 = f32[256,768]{1,0:T(8,128)} all-gather(f32[16,768]{1,0:T(8,128)S(1)} %bitcast_add_fusion.1), channel_id=1, replica_groups=mesh['pb'=16,'sa'=16] {'pb'}, dimensions={0}, use_global_device_ids=true | all-gather | bytes 835584 | tf_op jit(solution)/shard_map/all_gather | solution.py:101
  440.1 2.8 copy.41
  450.0 2.7 copy.44
  457.7 5.2 multiply_reduce_fusion.1
  467.0 90.3 %all-reduce.1 = (f32[768]{0:T(1024)}, f32[768]{0:T(1024)}) all-reduce(f32[768]{0:T(1024)S(1)} %multiply_reduce_fusion.1, f32[768]{0:T(1024)S(1)} %multiply_reduce_fusion), channel_id=1, replica_groups=mesh['pb'=16,'sa'=16] {'pb','sa'}, use_global_device_ids=true, to_apply=%region_17.0 | all-reduce | flops 1536 | bytes 12288 | tf_op jit(solution)/shard_map/psum | solution.py:139
  557.3 2.7 fusion.45
  561.6 55.2 %all-reduce.5.cloned.1.call-done = f32[768,192]{0,1:T(8,128)} async-done(((f32[768,192]{0,1:T(8,128)}), f32[768,192]{0,1:T(8,128)}) %all-reduce.5.cloned.1.call-update) | async-done | bytes 589840 | tf_op jit(solution)/shard_map/psum | solution.py:137
  616.8 132.7 %all-reduce.7.cloned.1.call-done = f32[768,192]{0,1:T(8,128)} async-done(((f32[768,192]{0,1:T(8,128)}), f32[768,192]{0,1:T(8,128)}) %all-reduce.7.cloned.1.call-update) | async-done | bytes 589840 | tf_op jit(solution)/shard_map/psum | solution.py:138
  (130 shorter events, 45.1 us)
Async XLA Ops:
  7.2 263.7 %copy-start = (bf16[768,192]{0,1:T(8,128)(2,1)S(1)}, bf16[768,192]{0,1:T(8,128)(2,1)}, u32[]{:S(2)}) copy-start(bf16[768,192]{0,1:T(8,128)(2,1)} %param.13) | copy-start | bytes 884740
  7.2 96.4 %all-gather.5.cloned.1.call-start = ((), (), s32[]{:S(2)}) async-start(), calls=%async_computation.2 | async-start | bytes 6684672 | tf_op jit(solution)/shard_map/all_gather | solution.py:88
  7.9 148.0 %all-gather.3.cloned.1.call-start = ((), (), s32[]{:S(2)}) async-start(), calls=%async_computation.1 | async-start | bytes 6684672 | tf_op jit(solution)/shard_map/all_gather | solution.py:87
  10.3 158.0 %copy-start.17 = (f32[16,256,1]{1,0,2:T(8,128)}, f32[16,256,1]{1,0,2:T(8,128)S(1)}, u32[]{:S(2)}) copy-start(f32[16,256,1]{1,0,2:T(8,128)S(1)} %get-tuple-element.26) | copy-start | bytes 49156
  107.7 55.4 %copy-start.20 = (f32[2,2,8,128]{3,1,2,0:T(2,128)}, f32[2,2,8,128]{3,1,2,0:T(2,128)S(1)}, u32[]{:S(2)}) copy-start(f32[2,2,8,128]{3,1,2,0:T(2,128)S(1)} %copy.38) | copy-start | bytes 49156
  155.9 4.6 copy-start.1
  240.8 25.5 %copy-start.22 = (f32[2,2,8,128]{3,1,2,0:T(2,128)S(1)}, f32[2,2,8,128]{3,1,2,0:T(2,128)}, u32[]{:S(2)}) copy-start(f32[2,2,8,128]{3,1,2,0:T(2,128)} %copy.36) | copy-start | bytes 49156
  240.8 25.5 %copy-start.24 = (f32[2,2,8,128]{3,1,2,0:T(2,128)S(1)}, f32[2,2,8,128]{3,1,2,0:T(2,128)}, u32[]{:S(2)}) copy-start(f32[2,2,8,128]{3,1,2,0:T(2,128)} %copy.37) | copy-start | bytes 49156
  240.8 25.5 %copy-start.28 = (f32[768]{0:T(1024)S(1)}, f32[768]{0:T(1024)}, u32[]{:S(2)}) copy-start(f32[768]{0:T(1024)} %param.15) | copy-start | bytes 9220
  247.2 184.8 %all-to-all-start = ((f32[16,16,768]{2,1,0:T(8,128)}), f32[16,16,768]{2,1,0:T(8,128)}, u32[]{:S(2)}, u32[]{:S(2)}) async-start(f32[16,16,768]{2,1,0:T(8,128)} %stack.2), calls=%async_computation | async-start | bytes 1572864 | tf_op jit(solution)/shard_map/all_to_all | solution.py:103
  266.3 350.6 %all-reduce.5.cloned.1.call-start = ((), (), s32[]{:S(2)}) async-start(), calls=%async_computation.3 | async-start | bytes 1179648 | tf_op jit(solution)/shard_map/psum | solution.py:137
  386.4 47.9 %copy-start.26 = (s32[256]{0:T(256)S(1)}, s32[256]{0:T(256)}, u32[]{:S(2)}) copy-start(s32[256]{0:T(256)} %all-reduce) | copy-start | bytes 3076
  432.0 5.3 copy-start.6
  432.0 7.2 copy-start.13
  440.1 5.5 slice-start.4
  447.9 301.6 %all-reduce.7.cloned.1.call-start = ((), (), s32[]{:S(2)}) async-start(), calls=%async_computation.4 | async-start | bytes 1179648 | tf_op jit(solution)/shard_map/psum | solution.py:138
  450.0 5.4 slice-start.2
  455.4 7.6 slice-start
  457.7 5.3 slice-start.1
  457.7 5.3 copy-start.11
  457.7 5.3 copy-start.16
  457.7 5.3 copy-start.21
  463.0 97.0 %copy-start.8 = (f32[256,768]{1,0:T(8,128)S(1)}, f32[256,768]{1,0:T(8,128)}, u32[]{:S(2)}) copy-start(f32[256,768]{1,0:T(8,128)} %copy-done.7) | copy-start | bytes 2359300
  463.1 97.0 %copy-start.15 = (f32[256,192]{1,0:T(8,128)S(1)}, f32[256,192]{1,0:T(8,128)}, u32[]{:S(2)}) copy-start(f32[256,192]{1,0:T(8,128)} %all_gather.22) | copy-start | bytes 589828
  (16 other events, 42.0 us)
Sparse Core Ops, SparseCore 0:
  10.5 93.0 all-gather.4
  105.5 50.4 all-gather.2
  448.0 168.7 all-reduce.4
  620.1 129.3 all-reduce.6
